TPU v7x, 128 devices: a whole 4x4x4 slice. The times are simulated.
128 devices in a mesh: fsdp: 32 (over y_hi, z, x), ctx: 4 (over y_lo, core).
Axes of the slice: x: 4, y: 4 (y_hi: 2, y_lo: 2; y = y_hi * 2 + y_lo), z: 4, core: 2. Of those that a mesh axis runs over, the one named last changes fastest.
Arguments:
- loaded: bfloat16 [32768, 12288], P(('fsdp', 'ctx')), may hold values from -6 to 6
- route: int32 [128, 32], P(('fsdp', 'ctx')), may hold values from 0 to 31, each once within a row
- doc_ids: int32 [32, 1024], P('fsdp'), may hold values from 0 to 7, never falling along the last dimension, each value on 1 to 512 neighbouring positions
- short_filter: float32 [7, 768], replicated, may hold values from -2 to 2
- medium_filter: bfloat16 [128, 256], replicated, may hold values from -0.5 to 0.5
- out_weight: bfloat16 [4096, 8192], P('fsdp', 'ctx'), may hold values from -0.09375 to 0.09375
Outputs:
- mixed: bfloat16 [32768, 8192], P(('fsdp', 'ctx'))
Inputs may be any that keep to these rules, and one draw needn't show every extreme that they name: Each row of route names every sequence 0 to 31 exactly once. `doc_ids`: along each sequence the document numbers never fall; each document spans 1 to 512 positions and one spans exactly 512.
All inputs are finite; a program needn't handle non-finite values.
Results may differ from a plain program's by a relative error of at most 0.0058.
Values may be sent and summed in bfloat16 or wider, within the bound.
A program may use at most 128 MiB of HBM per device.

v0:
```python
import jax
import jax.numpy as jnp
from jax import lax
from jax.sharding import PartitionSpec as P


def shifted_2(value, axis, steps):
    count = lax.axis_size(axis)
    first, last = (max(0, -steps), min(count, count - steps))
    return lax.ppermute(value, axis, [(source, source + steps) for source in range(first, last)])


def short_taps(extended, ext_ids, filter_full, count):
    taps = filter_full.shape[0]
    own_ids = ext_ids[taps - 1 : taps - 1 + count]
    summed = jnp.zeros((count, extended.shape[1]), jnp.float32)
    for offset in range(taps):
        shifted = extended[taps - 1 - offset : taps - 1 - offset + count].astype(jnp.float32)
        same_doc = (ext_ids[taps - 1 - offset : taps - 1 - offset + count] == own_ids).astype(
            jnp.float32
        )[:, None]
        summed = summed + filter_full[offset][None, :] * shifted * same_doc
    return summed


def medium_conv(gate_ext, mid_ids, medium_filter, group_size):
    taps = medium_filter.shape[0]
    groups = medium_filter.shape[1]
    block_rows = 32
    window = block_rows + taps - 1
    out_rows = gate_ext.shape[0] - (taps - 1)
    channels = gate_ext.shape[1]
    row_pos = jnp.arange(block_rows, dtype=jnp.int32)[:, None]
    col_pos = jnp.arange(window, dtype=jnp.int32)[None, :]
    offsets = row_pos - col_pos + taps - 1
    onehot = (offsets[:, :, None] == jnp.arange(taps, dtype=jnp.int32)[None, None, :]).astype(
        jnp.float32
    )
    table = jnp.einsum(
        "usk,kg->usg", onehot, medium_filter.astype(jnp.float32), precision=lax.Precision.HIGHEST
    ).astype(jnp.bfloat16)
    grouped = gate_ext.reshape(gate_ext.shape[0], groups, group_size)

    def one_block(block_index):
        first_row = block_index * block_rows
        window_rows = lax.dynamic_slice_in_dim(grouped, first_row, window, 0)
        window_ids = lax.dynamic_slice_in_dim(mid_ids, first_row, window, 0)
        target_ids = lax.dynamic_slice_in_dim(mid_ids, first_row + taps - 1, block_rows, 0)
        same_doc = (target_ids[:, None] == window_ids[None, :]).astype(jnp.bfloat16)
        matrix = table * same_doc[:, :, None]
        result = jnp.einsum("usg,sgc->ugc", matrix, window_rows, preferred_element_type=jnp.float32)
        return result.reshape(block_rows, channels)

    blocks_out = lax.map(one_block, jnp.arange(out_rows // block_rows, dtype=jnp.int32))
    return blocks_out.reshape(out_rows, channels)


def on_device(loaded, route, doc_ids, short_filter, medium_filter, out_weight):
    tok_rows = loaded.shape[0]
    wide = loaded.shape[1]
    channels = wide // 3
    fsdp_count = lax.axis_size("fsdp")
    short_len = short_filter.shape[0]
    medium_len = medium_filter.shape[0]
    group_size = wide // short_filter.shape[1]
    rim_depth = medium_len + short_len - 2
    inverse = jnp.argsort(route[0])
    send_blocks = jnp.take(
        loaded.reshape(fsdp_count, tok_rows // fsdp_count, wide), inverse, axis=0
    )
    owned = lax.all_to_all(send_blocks, "fsdp", split_axis=0, concat_axis=0, tiled=True).reshape(
        tok_rows, wide
    )
    doc_rows = doc_ids[0]
    base_pos = lax.axis_index("ctx") * tok_rows
    padded_ids = jnp.concatenate([jnp.full((rim_depth,), -1, jnp.int32), doc_rows], axis=0)
    ext_ids = lax.dynamic_slice_in_dim(padded_ids, base_pos, rim_depth + tok_rows, 0)
    short_full = jnp.repeat(short_filter, group_size, axis=1)
    feature_prev = shifted_2(owned[tok_rows - (short_len - 1) :], "ctx", 1)
    extended = jnp.concatenate([feature_prev, owned], axis=0)
    summed = short_taps(extended, ext_ids[medium_len - 1 :], short_full, tok_rows)
    query = summed[:, :channels]
    gate_in = (summed[:, channels : 2 * channels] * summed[:, 2 * channels :]).astype(jnp.bfloat16)
    gate_prev = shifted_2(gate_in[tok_rows - (medium_len - 1) :], "ctx", 1)
    gate_ext = jnp.concatenate([gate_prev, gate_in], axis=0)
    medium = medium_conv(gate_ext, ext_ids[short_len - 1 :], medium_filter, group_size)
    gated = (query * medium).astype(jnp.bfloat16)
    all_rows = lax.all_gather(gated, "ctx", axis=0, tiled=True)
    product = jnp.dot(
        all_rows,
        lax.all_gather(out_weight, "fsdp", axis=0, tiled=True),
        preferred_element_type=jnp.float32,
    )
    rounded = product.astype(jnp.bfloat16)
    return lax.all_to_all(rounded, "ctx", split_axis=0, concat_axis=1, tiled=True)


def solution(mesh):
    placed = (
        P(("fsdp", "ctx"), None),
        P(("fsdp", "ctx"), None),
        P("fsdp", None),
        P(),
        P(),
        P("fsdp", "ctx"),
    )
    return jax.shard_map(
        on_device, mesh=mesh, in_specs=placed, out_specs=P(("fsdp", "ctx"), None), check_vma=False
    )
```

profile of v0, /device:TPU:1, one launch (start us, length us, event | category | flops | bytes accessed | tf_op | source)
XLA Modules:
  0.0 571.3 jit_solution(15955327343027033988)
XLA Ops:
  6.5 2.3 sort.17
  8.9 6.4 %gather_fusion = bf16[32,8,12288]{2,1,0:T(8,128)(2,1)} fusion(bf16[32,8,12288]{2,1,0:T(8,128)(2,1)} %bitcast.27, s32[1024]{0:T(1024)S(1)} %pad_clamp_fusion), kind=kCustom, calls=%fused_computation | custom fusion | bytes 12583040 | tf_op jit(solution)/shard_map/jit(_take)/gather | solution.py:68
  15.2 6.1 %broadcast_select_fusion = bf16[32,8,12288]{2,1,0:T(8,128)(2,1)} fusion(bf16[32,8,12288]{2,1,0:T(8,128)(2,1)} %gather_fusion, pred[32]{0:T(512)(128)(4,1)S(1)} %compare_and_fusion), kind=kLoop, calls=%fused_computation.23 | loop fusion | flops 3145728 | bytes 12582944 | tf_op jit(solution)/shard_map/jit(_take)/select_n | solution.py:68
  21.4 11.6 %all-to-all-start = ((bf16[32,8,12288]{2,1,0:T(8,128)(2,1)}), bf16[32,8,12288]{2,1,0:T(8,128)(2,1)}, u32[]{:S(2)}, u32[]{:S(2)}) async-start(bf16[32,8,12288]{2,1,0:T(8,128)(2,1)} %broadcast_select_fusion), calls=%async_computation | async-start | bytes 12582912 | tf_op jit(solution)/shard_map/all_to_all | solution.py:71
  35.5 77.7 %all-to-all-done = bf16[32,8,12288]{2,1,0:T(8,128)(2,1)} async-done(((bf16[32,8,12288]{2,1,0:T(8,128)(2,1)}), bf16[32,8,12288]{2,1,0:T(8,128)(2,1)}, u32[]{:S(2)}, u32[]{:S(2)}) %all-to-all-start) | async-done | bytes 6291488 | tf_op jit(solution)/shard_map/all_to_all | solution.py:71
  113.2 1.0 slice.150
  114.2 7.6 %collective-permute-start = (bf16[6,12288]{1,0:T(8,128)(2,1)S(1)}, bf16[6,12288]{1,0:T(8,128)(2,1)S(1)}, u32[]{:S(2)}, u32[]{:S(2)}) collective-permute-start(bf16[6,12288]{1,0:T(8,128)(2,1)S(1)} %slice.150), channel_id=1, source_target_pairs={{0,1},{1,2},{2,3},{4,5},{5,6},{6,7},{8,9},{9,10},{10,11},{12,13},{... | collective-permute-start | bytes 442376 | tf_op jit(solution)/shard_map/ppermute | solution.py:10
  121.8 2.5 collective-permute-done
  124.3 26.5 %multiply_add_fusion = f32[256,12288]{1,0:T(8,128)S(1)} fusion(bf16[256,12288]{1,0:T(8,128)(2,1)} %bitcast.5, bf16[6,12288]{1,0:T(8,128)(2,1)S(1)} %collective-permute-done, f32[256]{0:T(256)S(1)} %get-tuple-element.168, f32[12288]{0:T(1024)S(1)} %broadcast_in_dim.85, f32[256]{0:T(256)S(1)} %get-tuple-element.169, f32[12288]{0:T(1024)S(1)} %broadcast_in_dim.83, ...), kind=kLoop, calls=%fused_computation.13 | loop fusion | flops 138412032 | bytes 19372032 | tf_op jit(solution)/shard_map/add | solution.py:22
  150.8 4.6 copy-done.2
  156.2 4.4 collective-permute-start.1
  160.6 2.8 fusion.13
  163.4 7.6 %copy.15 = bf16[32,159,256]{1,0,2:T(8,128)(2,1)} copy(bf16[32,159,256]{2,1,0:T(8,128)(2,1)} %fusion.13) | data formatting | bytes 5210112 | tf_op jit(solution)/shard_map/while | solution.py:54
  171.0 1.3 collective-permute-done.1
  172.3 3.5 pad_maximum_fusion.1
  175.7 4.6 copy.14
  180.4 57.0 %while.14 = (s32[]{:T(128)}, f32[8,32,4096]{2,1,0:T(8,128)}, s32[8]{0:T(128)S(1)}, bf16[383,256,16]{0,2,1:T(8,128)(2,1)}, s32[383]{0:T(512)S(1)}, /*index=5*/bf1...) while((s32[]{:T(128)}, f32[8,32,4096]{2,1,0:T(8,128)}, ...), condition=%wide.region_2.3_spmd, body=%wide.region_1.2_spmd.sunk | while | flops 42993608 | bytes 8936285 | solution.py:54
  181.9 4.4 fusion.23
  186.8 0.8 constant_dynamic-update-slice_fusion.2
  189.1 4.4 fusion.23
  196.4 4.4 fusion.23
  203.7 4.4 fusion.23
  211.0 4.1 fusion.23
  217.9 4.1 fusion.23
  224.9 4.1 fusion.23
  231.9 4.1 fusion.23
  237.4 5.4 fusion.11
  243.5 87.7 %all-gather.3.cloned.1.call-done = bf16[1024,4096]{1,0:T(8,128)(2,1)} async-done(((bf16[256,4096]{1,0:T(8,128)(2,1)}), bf16[1024,4096]{1,0:T(8,128)(2,1)}) %all-gather.3.cloned.1.call-update) | async-done | bytes 8388624 | tf_op jit(solution)/shard_map/all_gather | solution.py:88
  331.2 157.1 %all-gather.5.cloned.1.call-done = bf16[4096,2048]{1,0:T(8,128)(2,1)} async-done(((bf16[128,2048]{1,0:T(8,128)(2,1)}), bf16[4096,2048]{1,0:T(8,128)(2,1)}) %all-gather.5.cloned.1.call-update) | async-done | bytes 16777232 | tf_op jit(solution)/shard_map/all_gather | solution.py:91
  488.3 22.7 %convolution_convert_fusion = bf16[1024,2048]{1,0:T(8,128)(2,1)S(1)} fusion(bf16[1024,4096]{1,0:T(8,128)(2,1)} %all-gather.3.cloned.1.call-done, bf16[4096,2048]{1,0:T(8,128)(2,1)} %all-gather.5.cloned.1.call-done), kind=kOutput, calls=%fused_computation.28 | convolution fusion | flops 17181966336 | bytes 29360128 | tf_op jit(solution)/shard_map/dot_general | solution.py:89
  511.0 51.2 %all_to_all.24 = bf16[4,256,2048]{2,1,0:T(8,128)(2,1)S(1)} all-to-all(bf16[4,256,2048]{2,1,0:T(8,128)(2,1)S(1)} %bitcast.28), channel_id=1, replica_groups=mesh['fsdp'=32,'ctx'=4] {'ctx'}, dimensions={0} | all-to-all | bytes 8388608 | tf_op jit(solution)/shard_map/all_to_all | solution.py:95
  562.1 2.3 copy.20
  (87 shorter events, 21.3 us)
Async XLA Ops:
  6.5 154.1 %copy-start = (bf16[128,256]{1,0:T(8,128)(2,1)S(1)}, bf16[128,256]{1,0:T(8,128)(2,1)}, u32[]{:S(2)}) copy-start(bf16[128,256]{1,0:T(8,128)(2,1)} %param.12) | copy-start | bytes 196612
  21.4 11.6 %copy-start.3 = (f32[7,768]{1,0:T(8,128)S(1)}, f32[7,768]{1,0:T(8,128)}, u32[]{:S(2)}) copy-start(f32[7,768]{1,0:T(8,128)} %param.11) | copy-start | bytes 64516
  21.4 14.0 %copy-start.4 = (s32[1,1024]{1,0:T(1,128)S(1)}, s32[1,1024]{1,0:T(1,128)}, u32[]{:S(2)}) copy-start(s32[1,1024]{1,0:T(1,128)} %param.10) | copy-start | bytes 12292
  21.4 91.8 %all-to-all-start = ((bf16[32,8,12288]{2,1,0:T(8,128)(2,1)}), bf16[32,8,12288]{2,1,0:T(8,128)(2,1)}, u32[]{:S(2)}, u32[]{:S(2)}) async-start(bf16[32,8,12288]{2,1,0:T(8,128)(2,1)} %broadcast_select_fusion), calls=%async_computation | async-start | bytes 12582912 | tf_op jit(solution)/shard_map/all_to_all | solution.py:71
  32.9 298.2 %all-gather.3.cloned.1.call-start = ((), (), s32[]{:S(2)}) async-start(), calls=%async_computation.2 | async-start | bytes 10485760 | tf_op jit(solution)/shard_map/all_gather | solution.py:88
  114.2 10.2 %collective-permute-start = (bf16[6,12288]{1,0:T(8,128)(2,1)S(1)}, bf16[6,12288]{1,0:T(8,128)(2,1)S(1)}, u32[]{:S(2)}, u32[]{:S(2)}) collective-permute-start(bf16[6,12288]{1,0:T(8,128)(2,1)S(1)} %slice.150), channel_id=1, source_target_pairs={{0,1},{1,2},{2,3},{4,5},{5,6},{6,7},{8,9},{9,10},{10,11},{12,13},{... | collective-permute-start | bytes 442376 | tf_op jit(solution)/shard_map/ppermute | solution.py:10
  150.8 4.6 copy-start.2
  156.2 16.1 %collective-permute-start.1 = (bf16[127,4096]{1,0:T(8,128)(2,1)S(1)}, bf16[127,4096]{1,0:T(8,128)(2,1)}, u32[]{:S(2)}, u32[]{:S(2)}) collective-permute-start(bf16[127,4096]{1,0:T(8,128)(2,1)S(1)} %slice.164), channel_id=1, source_target_pairs={{0,1},{1,2},{2,3},{4,5},{5,6},{6,7},{8,9},{9,10},{10,11},{12,13},{... | collective-permute-start | bytes 3121160 | tf_op jit(solution)/shard_map/ppermute | solution.py:10
  242.8 245.5 %all-gather.5.cloned.1.call-start = ((), (), s32[]{:S(2)}) async-start(), calls=%async_computation.3 | async-start | bytes 17301504 | tf_op jit(solution)/shard_map/all_gather | solution.py:91
  510.9 53.5 %copy-start.1 = (bf16[128,256]{1,0:T(8,128)(2,1)S(1)}, bf16[128,256]{1,0:T(8,128)(2,1)}, u32[]{:S(2)}) copy-start(bf16[128,256]{1,0:T(8,128)(2,1)} %param.12) | copy-start | bytes 196612
Sparse Core Ops, SparseCore 0:
  242.9 88.2 all-gather.2
  334.2 153.9 all-gather.4
where the time goes:
time: 572 us; the launch traced here: 571 us
  waiting for transfers between devices  327 us (57%)
  matrix products  59.3 us (10%)
  blocking collectives  51.2 us (9%)
  local copies, waits for them, and re-layouts  46.6 us (8%)
  other arithmetic  44.9 us (8%)
  starting transfers between devices  23.8 us (4%)
  between operations  13.6 us (2%)
    all_gather x1, waiting for transfers between devices, on_device(): lax.all_gather(out_weight, 'fsdp', axis=0, tiled=True)  157 us
    all_gather x1, waiting for transfers between devices, on_device(): all_rows = lax.all_gather(gated, 'ctx', axis=0, tiled=True)  87.7 us
    all_to_all x1, waiting for transfers between devices, on_device(): lax.all_to_all(send_blocks, 'fsdp', split_axis=0, concat_axis=0, tiled=True)  77.7 us
    all_to_all x1, blocking collectives, on_device(): lax.all_to_all(rounded, 'ctx', split_axis=0, concat_axis=1, tiled=True)  51.2 us
    dot_general x8, matrix products, one_block(): jnp.einsum('usg,sgc->ugc', matrix, window_rows, preferred_element_type=jn...  33.9 us
    add x1, other arithmetic, short_taps(): summed = summed + filter_full[offset][None, :] * shifted * same_doc  26.5 us
    dot_general x1, matrix products, on_device(): jnp.dot(all_rows, lax.all_gather(out_weight, 'fsdp', axis=0, tiled=True),...  22.7 us
    ppermute x2, starting transfers between devices, shifted_2(): lax.ppermute(value, axis, [(source, source + steps) for source in range(f...  12 us
  transfers between devices with their start and end apart: 5, of which 5 were waited for; matrix products, arithmetic and copies ran while one was open for 2% of the time, Pallas kernels for 0%

commit v1 on v0

v1 whole, which is shorter than its diff:
```python
import functools

import jax
import jax.numpy as jnp
from jax import lax
from jax.experimental import pallas as pl
from jax.experimental.pallas import tpu as pltpu
from jax.sharding import PartitionSpec as P

MESH = pl.DeviceIdType.MESH
VMEM_LIMIT = 66_000_000
RING = 4
WAVES = 4
TILE = 256
BLOCK = 128
GROUP = 16
TAPS = 7
CHUNK = 512
BUFFERS = 4


def pick_kernel(order, loaded, picked, held, load_sem, store_sem):
    blocks = loaded.shape[0]

    def load(i, start):
        copy = pltpu.make_async_copy(loaded.at[order[i]], held.at[i], load_sem.at[i])
        copy.start() if start else copy.wait()

    def store(i, start):
        copy = pltpu.make_async_copy(held.at[i], picked.at[i], store_sem.at[i])
        copy.start() if start else copy.wait()

    @pl.loop(0, blocks)
    def _(i):
        load(i, True)

    @pl.loop(0, blocks)
    def _(i):
        load(i, False)
        store(i, True)

    @pl.loop(0, blocks)
    def _(i):
        store(i, False)


def pick_blocks(order, loaded):
    blocks, rows, wide = loaded.shape
    return pl.pallas_call(
        pick_kernel,
        out_shape=jax.ShapeDtypeStruct(loaded.shape, loaded.dtype),
        in_specs=[
            pl.BlockSpec(memory_space=pltpu.SMEM),
            pl.BlockSpec(memory_space=pl.ANY),
        ],
        out_specs=pl.BlockSpec(memory_space=pl.ANY),
        scratch_shapes=[
            pltpu.VMEM((blocks, rows, wide), loaded.dtype),
            pltpu.SemaphoreType.DMA((blocks,)),
            pltpu.SemaphoreType.DMA((blocks,)),
        ],
        compiler_params=pltpu.CompilerParams(vmem_limit_bytes=VMEM_LIMIT),
        name="pick_blocks",
    )(order, loaded)


def band_kernel(base_ref, mask_ref, out_ref):
    def one(j, carry):
        row = jnp.broadcast_to(base_ref[pl.ds(j, 1), :], (BLOCK, 2 * BLOCK))
        band = pltpu.roll(row, 0, 1, stride=1, stride_axis=0)
        start = pl.multiple_of(j * BLOCK, BLOCK)
        for b in range(2):
            out_ref[0, b, pl.ds(start, BLOCK), :] = (band * mask_ref[b]).astype(jnp.bfloat16)
        return carry

    lax.fori_loop(0, GROUP, one, 0)


def build_bands(base, mask):
    groups = base.shape[0]
    tiles = groups // GROUP
    return pl.pallas_call(
        band_kernel,
        out_shape=jax.ShapeDtypeStruct((tiles, 2, GROUP * BLOCK, 2 * BLOCK), jnp.bfloat16),
        grid=(tiles,),
        in_specs=[
            pl.BlockSpec((GROUP, 2 * BLOCK), lambda t: (t, 0)),
            pl.BlockSpec((2, BLOCK, 2 * BLOCK), lambda t: (0, 0, 0)),
        ],
        out_specs=pl.BlockSpec((1, 2, GROUP * BLOCK, 2 * BLOCK), lambda t: (t, 0, 0, 0)),
        cost_estimate=pl.CostEstimate(
            flops=groups * BLOCK * BLOCK * 8, bytes_accessed=groups * BLOCK * BLOCK * 8, transcendentals=0
        ),
        name="build_bands",
    )(base, mask)


def mixer_kernel(
    owned, bands, short_mask, short_full, weight, out,
    w_all, gated, staged, rows, feat, gate, xk, band_buf,
    ys, yr, d1s, d1r, d2s, d2r, e1s, e1r, e2s, e2r,
    fs, fr, hs, hr, ns, nr, ss, sr, gs, gr, cs, cr, ls, bs, os,
):
    fsdp, ctx = lax.axis_index("fsdp"), lax.axis_index("ctx")
    yh, zc, xc = fsdp // (RING * RING), (fsdp // RING) % RING, fsdp % RING
    sib, nb = (fsdp, ctx ^ 1), (fsdp, ctx ^ 2)
    after, before = (fsdp, (ctx + 1) % 4), (fsdp, (ctx + 3) % 4)
    partner = ((1 - yh) * RING * RING + zc * RING + xc, ctx)
    channels = gated.shape[2]
    tiles = channels // TILE
    chunks = channels // CHUNK
    tok = owned.shape[0]

    def coords(h):
        return (xc, zc) if h == 0 else (zc, xc)

    def dev(h, a, b):
        a, b = (a + RING) % RING, (b + RING) % RING
        z, x = (b, a) if h == 0 else (a, b)
        return (yh * RING * RING + z * RING + x, ctx)

    def piece(w, h, y, a, b):
        a, b = (a + RING) % RING, (b + RING) % RING
        z, x = (b, a) if h == 0 else (a, b)
        return w_all.at[w, h, y, z, x]

    def panel(w, h, y, b):
        b = (b + RING) % RING
        if h == 0:
            return w_all.at[w, h, y, b]
        return w_all.at[w, h, y, :, b]

    def panels(w, h, b):
        b = (b + RING) % RING
        if h == 0:
            return w_all.at[w, h, :, b]
        return w_all.at[w, h, :, :, b]

    def shard(w, h):
        return weight.at[:, pl.ds(w * CHUNK + h * TILE, TILE)]

    def remote(src, dst, send, recv, to):
        return pltpu.make_async_remote_copy(
            src_ref=src, dst_ref=dst, send_sem=send, recv_sem=recv, device_id=to, device_id_type=MESH
        )

    halves = [(w, h) for w in range(WAVES) for h in range(2)]
    ways = ((0, 1), (1, -1))

    def y_copy(w, h):
        a, b = coords(h)
        return remote(shard(w, h), piece(w, h, yh, a, b), ys.at[w, h], yr.at[w, h], partner)

    def y_got(w, h):
        a, b = coords(h)
        return remote(shard(w, h), piece(w, h, 1 - yh, a, b), ys.at[w, h], yr.at[w, h], partner)

    def d1_copy(w, h, d, step, other):
        a, b = coords(h)
        y = 1 - yh if other else yh
        src = piece(w, h, y, a, b) if other else shard(w, h)
        return remote(src, piece(w, h, y, a, b), d1s.at[w, h, d, other], d1r.at[w, h, d, other], dev(h, a + step, b))

    def d1_got(w, h, d, step, other):
        a, b = coords(h)
        y = 1 - yh if other else yh
        dst = piece(w, h, y, a - step, b)
        return remote(dst, dst, d1s.at[w, h, d, other], d1r.at[w, h, d, other], dev(h, a + step, b))

    def d2_copy(w, h, d, step):
        a, b = coords(h)
        ref = piece(w, h, d, a - step, b)
        return remote(ref, ref, d2s.at[w, h, d], d2r.at[w, h, d], dev(h, a + step, b))

    def d2_got(w, h, d, step):
        a, b = coords(h)
        ref = piece(w, h, d, a - 2 * step, b)
        return remote(ref, ref, d2s.at[w, h, d], d2r.at[w, h, d], dev(h, a + step, b))

    def e1_copy(w, h, d, step):
        a, b = coords(h)
        return remote(panels(w, h, b), panels(w, h, b), e1s.at[w, h, d], e1r.at[w, h, d], dev(h, a, b + step))

    def e1_got(w, h, d, step):
        a, b = coords(h)
        ref = panels(w, h, b - step)
        return remote(ref, ref, e1s.at[w, h, d], e1r.at[w, h, d], dev(h, a, b + step))

    def e2_copy(w, h, d, step):
        a, b = coords(h)
        ref = panel(w, h, d, b - step)
        return remote(ref, ref, e2s.at[w, h, d], e2r.at[w, h, d], dev(h, a, b + step))

    def e2_got(w, h, d, step):
        a, b = coords(h)
        ref = panel(w, h, d, b - 2 * step)
        return remote(ref, ref, e2s.at[w, h, d], e2r.at[w, h, d], dev(h, a, b + step))

    def own_shard(w, h):
        a, b = coords(h)
        return pltpu.make_async_copy(shard(w, h), piece(w, h, yh, a, b), os.at[w, h])

    def feat_copy():
        return remote(owned.at[pl.ds(tok - 8, 8)], feat, fs, fr, after)

    def halo_copy(t):
        return remote(
            gate.at[t, pl.ds(tok, BLOCK)], gate.at[t, pl.ds(0, BLOCK)], hs.at[t], hr.at[t], after
        )

    def part(c, k):
        return gated.at[c, :, pl.ds(pl.multiple_of(k * CHUNK, CHUNK), CHUNK)]

    def near_copy(k):
        return remote(part(ctx, k), part(ctx, k), ss.at[k], sr.at[k], sib)

    def near_got(k):
        return remote(part(ctx ^ 1, k), part(ctx ^ 1, k), ss.at[k], sr.at[k], sib)

    def far_copy(k):
        return remote(part(ctx, k), part(ctx, k), ns.at[k], nr.at[k], nb)

    def far_got(k):
        return remote(part(ctx ^ 2, k), part(ctx ^ 2, k), ns.at[k], nr.at[k], nb)

    def hand_copy(k):
        return remote(part(ctx ^ 2, k), part(ctx ^ 2, k), gs.at[k], gr.at[k], sib)

    def hand_got(k):
        return remote(part(ctx ^ 3, k), part(ctx ^ 3, k), gs.at[k], gr.at[k], sib)

    def out_at(c, w, h):
        start = pl.multiple_of(c * (WAVES * CHUNK) + w * CHUNK + h * TILE, TILE)
        return out.at[:, pl.ds(start, TILE)]

    def c_copy(w, h, c):
        return remote(staged.at[w, h, c], out_at(ctx, w, h), cs.at[w, h, c], cr.at[w, h, ctx], (fsdp, c))

    def c_got(w, h, c):
        return remote(staged.at[w, h, c], out_at(c, w, h), cs.at[w, h, c], cr.at[w, h, c], (fsdp, c))

    def c_own(w, h):
        return pltpu.make_async_copy(staged.at[w, h, ctx], out_at(ctx, w, h), cs.at[w, h, ctx])

    def band_copy(t, b):
        slot = (2 * t + b) % BUFFERS
        return pltpu.make_async_copy(bands.at[t, b], band_buf.at[slot], bs.at[slot])

    barrier = pltpu.get_barrier_semaphore()
    friends = [sib, nb, (fsdp, ctx ^ 3), partner]
    friends += [dev(0, xc + 1, zc), dev(0, xc - 1, zc), dev(0, xc, zc + 1), dev(0, xc, zc - 1)]
    for friend in friends:
        pl.semaphore_signal(barrier, inc=1, device_id=friend, device_id_type=MESH)
    pl.semaphore_wait(barrier, len(friends))

    feat_copy().start()
    rows_copy = pltpu.make_async_copy(owned, rows, ls)
    rows_copy.start()
    for i in range(BUFFERS):
        band_copy(i // 2, i % 2).start()
    for w, h in halves:
        y_copy(w, h).start()
        for d, step in ways:
            d1_copy(w, h, d, step, 0).start()
    for w, h in halves:
        own_shard(w, h).start()
    rows_copy.wait()
    feat_copy().wait_recv()

    lane_group = lax.broadcasted_iota(jnp.int32, (BLOCK, TILE), 1) // GROUP

    def expand(slot, column):
        xk[slot, pl.ds(0, 8), :] = feat[:, pl.ds(column, TILE)].astype(jnp.float32)
        xk[slot, pl.ds(8, tok), :] = rows[:, pl.ds(column, TILE)].astype(jnp.float32)

    def short(slot, column, b, lanes):
        total = None
        for i in range(TAPS):
            tap = short_full[i, pl.ds(pl.multiple_of(column + lanes, BLOCK), BLOCK)][None, :]
            term = xk[slot, pl.ds(8 + b * BLOCK - i, BLOCK), lanes : lanes + BLOCK] * tap
            if i > 0:
                term = term * short_mask[i - 1, b * BLOCK : (b + 1) * BLOCK, :]
            total = term if total is None else total + term
        return total

    def make_gate(t):
        key = pl.multiple_of(channels + t * TILE, TILE)
        value = pl.multiple_of(2 * channels + t * TILE, TILE)
        expand(0, key)
        expand(1, value)
        for b in range(2):
            for lanes in range(0, TILE, BLOCK):
                product = short(0, key, b, lanes) * short(1, value, b, lanes)
                gate[t, pl.ds((b + 1) * BLOCK, BLOCK), lanes : lanes + BLOCK] = product.astype(jnp.bfloat16)
        halo_copy(t).start()

    def convolve(t):
        query = pl.multiple_of(t * TILE, TILE)
        expand(2, query)
        halo_copy(t).wait_recv()
        for b in range(2):
            band_copy(t, b).wait()
            slot = (2 * t + b) % BUFFERS
            spread = jnp.dot(
                band_buf[slot], gate[t, pl.ds(b * BLOCK, 2 * BLOCK), :], preferred_element_type=jnp.float32
            )
            medium = spread[0:BLOCK]
            for j in range(1, GROUP):
                medium = jnp.where(lane_group == j, spread[j * BLOCK : (j + 1) * BLOCK], medium)
            for lanes in range(0, TILE, BLOCK):
                done = short(2, query, b, lanes) * medium[:, lanes : lanes + BLOCK]
                start = pl.multiple_of(query + lanes, BLOCK)
                gated[ctx, b * BLOCK : (b + 1) * BLOCK, pl.ds(start, BLOCK)] = done.astype(jnp.bfloat16)

            @pl.when(t + BUFFERS // 2 < tiles)
            def _():
                band_copy(t + BUFFERS // 2, b).start()

    lead = 2
    for t in range(lead):
        make_gate(t)

    for w, h in halves:
        y_got(w, h).wait_recv()
        for d, step in ways:
            d1_copy(w, h, d, step, 1).start()

    def weight_two():
        for w, h in halves:
            for d, step in ways:
                d1_got(w, h, d, step, 0).wait_recv()
                d1_got(w, h, d, step, 1).wait_recv()
                d2_copy(w, h, d, step).start()

    def weight_three(w):
        for h in range(2):
            own_shard(w, h).wait()
            for d, step in ways:
                d2_got(w, h, d, step).wait_recv()
        for h in range(2):
            for d, step in ways:
                e1_copy(w, h, d, step).start()

    def weight_four(w):
        for h in range(2):
            for d, step in ways:
                e1_got(w, h, d, step).wait_recv()
                e2_copy(w, h, d, step).start()

    def weight_done(w):
        for h in range(2):
            for d, step in ways:
                e2_got(w, h, d, step).wait_recv()

    def hand_on(k):
        far_got(k).wait_recv()
        hand_copy(k).start()

    def one_chunk(k, carry):
        def one_tile(i, carry):
            t = 2 * k + i

            @pl.when(t + lead < tiles)
            def _():
                make_gate(t + lead)

            convolve(t)
            return carry

        lax.fori_loop(0, 2, one_tile, 0)
        far_copy(k).start()
        near_copy(k).start()

        @pl.when(k == 1)
        def _():
            weight_two()

        @pl.when(k == 3)
        def _():
            weight_three(0)
            weight_three(1)

        @pl.when(k == 5)
        def _():
            weight_three(2)

        return carry

    lax.fori_loop(0, chunks, one_chunk, 0)

    for k in range(4):
        hand_on(k)
    weight_four(0)
    weight_three(3)
    hand_on(4)
    weight_four(1)
    hand_on(5)
    hand_on(6)
    weight_four(2)
    hand_on(7)
    for k in range(chunks):
        near_got(k).wait_recv()
        hand_got(k).wait_recv()

    mine = ctx // 2

    def multiply(w):
        def one_half(h, carry):
            cols = w_all[w, h].reshape(channels, TILE)
            for far in (1, 0):
                base = 2 * ((mine + far) % 2)
                lhs = gated[pl.ds(base, 2)].reshape(2 * tok, channels)
                product = jnp.dot(lhs, cols, preferred_element_type=jnp.float32)
                staged[w, h, pl.ds(base, 2)] = product.astype(jnp.bfloat16).reshape(2, tok, TILE)
                if far:
                    c_copy(w, h, base).start()
                    c_copy(w, h, base + 1).start()
                else:
                    c_copy(w, h, ctx ^ 1).start()
                    c_own(w, h).start()
            return carry

        lax.fori_loop(0, 2, one_half, 0)

    for w in range(WAVES):
        weight_done(w)
        multiply(w)
        if w == 0:
            weight_four(3)

    feat_copy().wait_send()
    for w, h in halves:
        y_copy(w, h).wait_send()
        for d, step in ways:
            for other in range(2):
                d1_copy(w, h, d, step, other).wait_send()
            d2_copy(w, h, d, step).wait_send()
            e1_copy(w, h, d, step).wait_send()
            e2_copy(w, h, d, step).wait_send()
    for t in range(tiles):
        halo_copy(t).wait_send()
    for k in range(chunks):
        far_copy(k).wait_send()
        near_copy(k).wait_send()
        hand_copy(k).wait_send()
    for w, h in halves:
        c_own(w, h).wait()
        for flip in (1, 2, 3):
            c_copy(w, h, ctx ^ flip).wait_send()
            c_got(w, h, ctx ^ flip).wait_recv()


def mix(owned, bands, short_mask, short_full, weight):
    tok, wide = owned.shape
    channels = wide // 3
    depth, columns = weight.shape
    tiles, chunks = channels // TILE, channels // CHUNK
    dma = pltpu.SemaphoreType.DMA
    vmem, anywhere = pl.BlockSpec(memory_space=pltpu.VMEM), pl.BlockSpec(memory_space=pl.ANY)
    return pl.pallas_call(
        mixer_kernel,
        out_shape=jax.ShapeDtypeStruct((tok, 4 * columns), jnp.bfloat16),
        in_specs=[anywhere, anywhere, vmem, vmem, anywhere],
        out_specs=anywhere,
        scratch_shapes=[
            pltpu.VMEM((WAVES, 2, 2, RING, RING, depth, TILE), jnp.bfloat16),
            pltpu.VMEM((4, tok, channels), jnp.bfloat16),
            pltpu.VMEM((WAVES, 2, 4, tok, TILE), jnp.bfloat16),
            pltpu.VMEM((tok, wide), jnp.bfloat16),
            pltpu.VMEM((8, wide), jnp.bfloat16),
            pltpu.VMEM((tiles, tok + BLOCK, TILE), jnp.bfloat16),
            pltpu.VMEM((3, tok + 8, TILE), jnp.float32),
            pltpu.VMEM((BUFFERS, GROUP * BLOCK, 2 * BLOCK), jnp.bfloat16),
            dma((WAVES, 2)), dma((WAVES, 2)),
            dma((WAVES, 2, 2, 2)), dma((WAVES, 2, 2, 2)),
            dma((WAVES, 2, 2)), dma((WAVES, 2, 2)),
            dma((WAVES, 2, 2)), dma((WAVES, 2, 2)),
            dma((WAVES, 2, 2)), dma((WAVES, 2, 2)),
            dma(()), dma(()),
            dma((tiles,)), dma((tiles,)),
            dma((chunks,)), dma((chunks,)),
            dma((chunks,)), dma((chunks,)),
            dma((chunks,)), dma((chunks,)),
            dma((WAVES, 2, 4)), dma((WAVES, 2, 4)),
            dma(()), dma((BUFFERS,)), dma((WAVES, 2)),
        ],
        compiler_params=pltpu.CompilerParams(
            vmem_limit_bytes=VMEM_LIMIT, collective_id=0, has_side_effects=True
        ),
        name="mixer",
    )(owned, bands, short_mask, short_full, weight)


def on_device(loaded, route, doc_ids, short_filter, medium_filter, out_weight):
    tok, wide = loaded.shape
    fsdp_count = lax.axis_size("fsdp")
    blk = tok // fsdp_count
    group = wide // short_filter.shape[1]
    taps = medium_filter.shape[0]

    slots = jnp.arange(fsdp_count, dtype=jnp.int32)
    order = jnp.sum(jnp.where(route[0][None, :] == slots[:, None], slots[None, :], 0), axis=1).astype(jnp.int32)
    picked = pick_blocks(order, loaded.reshape(fsdp_count, blk, wide))
    owned = lax.all_to_all(picked, "fsdp", split_axis=0, concat_axis=0, tiled=True).reshape(tok, wide)

    ids = jnp.concatenate([jnp.full((BLOCK,), -1, jnp.int32), doc_ids[0]], axis=0)
    near_ids = lax.dynamic_slice_in_dim(ids, lax.axis_index("ctx") * tok, tok + BLOCK, 0)
    own_ids = near_ids[BLOCK:]
    short_mask = jnp.stack(
        [
            jnp.broadcast_to((near_ids[BLOCK - i : BLOCK - i + tok] == own_ids)[:, None], (tok, BLOCK))
            for i in range(1, TAPS)
        ]
    ).astype(jnp.float32)
    short_full = jnp.pad(jnp.repeat(short_filter, group, axis=1), ((0, 1), (0, 0)))
    mask = jnp.stack(
        [
            own_ids[b * BLOCK : (b + 1) * BLOCK, None] == near_ids[None, b * BLOCK : (b + 2) * BLOCK]
            for b in range(2)
        ]
    ).astype(jnp.float32)
    base = jnp.pad(medium_filter[::-1].T.astype(jnp.float32), ((0, 0), (1, 2 * BLOCK - 1 - taps)))
    bands = build_bands(base, mask)
    return mix(owned, bands, short_mask, short_full, out_weight)


def solution(mesh):
    placed = (
        P(("fsdp", "ctx"), None),
        P(("fsdp", "ctx"), None),
        P("fsdp", None),
        P(),
        P(),
        P("fsdp", "ctx"),
    )
    return jax.shard_map(
        on_device, mesh=mesh, in_specs=placed, out_specs=P(("fsdp", "ctx"), None), check_vma=False
    )
```

time: 572 us -> 254 us (0.44)
  waiting for transfers between devices: 327 us -> 43.7 us
  Pallas kernels: 0 us -> 185 us
  matrix products: 59.3 us -> 0 us
  blocking collectives: 51.2 us -> 0 us
  other arithmetic: 44.9 us -> 3.97 us
  local copies, waits for them, and re-layouts: 46.6 us -> 9.09 us
  between operations: 13.6 us -> 0.15 us
  starting transfers between devices: 23.8 us -> 11.6 us
    all_gather x2 -> x0, waiting for transfers between devices: 245 us -> none  [the longest x1 157 us: on_device(): lax.all_gather(out_weight, 'fsdp', axis=0, tiled=True)]
    pallas_call x0 -> x3, Pallas kernels: none -> 185 us  [the longest x1 149 us: mix(): pl.pallas_call(mixer_kernel, out_shape=jax.ShapeDtypeStruct((tok, 4 * col...]
    dot_general x10 -> x0, matrix products: 59.3 us -> none  [the longest x8 33.9 us: one_block(): jnp.einsum('usg,sgc->ugc', matrix, window_rows, preferred_element_type=jn...]
    all_to_all x1 -> x0, blocking collectives: 51.2 us -> none  [on_device(): lax.all_to_all(rounded, 'ctx', split_axis=0, concat_axis=1, tiled=True)]
    all_to_all x1, waiting for transfers between devices: 77.7 us -> 43.7 us  [on_device(): lax.all_to_all(picked, 'fsdp', split_axis=0, concat_axis=0, tiled=True)]
    add x1 -> x0, other arithmetic: 26.5 us -> none  [short_taps(): summed = summed + filter_full[offset][None, :] * shifted * same_doc]
    ppermute x2 -> x0, starting transfers between devices: 12 us -> none  [shifted_2(): lax.ppermute(value, axis, [(source, source + steps) for source in range(f...]
    dynamic_update_slice x16 -> x0, local copies, waits for them, and re-layouts: 11.5 us -> none  [medium_conv(): lax.map(one_block, jnp.arange(out_rows // block_rows, dtype=jnp.int32))]
  transfers between devices with their start and end apart: 5 -> 1, of which waited for: 5 -> 1; matrix products, arithmetic and copies ran while one was open for 2% -> 3% of each run, Pallas kernels for 0% -> 12%
where the time goes in v1:
time: 254 us; the launch traced here: 253 us
  Pallas kernels  185 us (73%)
  waiting for transfers between devices  43.7 us (17%)
  starting transfers between devices  11.6 us (5%)
  local copies, waits for them, and re-layouts  9.09 us (4%)
  other arithmetic  3.97 us (2%)
    pallas_call x1, Pallas kernels, mix(): pl.pallas_call(mixer_kernel, out_shape=jax.ShapeDtypeStruct((tok, 4 * col...  149 us
    all_to_all x1, waiting for transfers between devices, on_device(): lax.all_to_all(picked, 'fsdp', split_axis=0, concat_axis=0, tiled=True)  43.7 us
    pallas_call x1, Pallas kernels, build_bands(): pl.pallas_call(band_kernel, out_shape=jax.ShapeDtypeStruct((tiles, 2, GRO...  29.4 us
    all_to_all x1, starting transfers between devices, on_device(): lax.all_to_all(picked, 'fsdp', split_axis=0, concat_axis=0, tiled=True)  11.6 us
    pallas_call x1, Pallas kernels, pick_blocks(): pl.pallas_call(pick_kernel, out_shape=jax.ShapeDtypeStruct(loaded.shape,...  6.3 us
    unnamed x13, local copies, waits for them, and re-layouts  5.34 us
  transfers between devices with their start and end apart: 1, of which 1 were waited for; matrix products, arithmetic and copies ran while one was open for 3% of the time, Pallas kernels for 12%

profile of v1, /device:TPU:1, one launch (start us, length us, event | category | flops | bytes accessed | tf_op | source)
XLA Modules:
  0.0 253.4 jit_solution(8097744494860696733)
XLA Ops:
  0.0 1.3 select_reduce_fusion.order
  1.3 6.3 %pick_blocks.1 = bf16[32,8,12288]{2,1,0:T(8,128)(2,1)} custom-call(s32[32]{0:T(128)} %select_reduce_fusion.order, bf16[32,8,12288]{2,1,0:T(8,128)(2,1)} %bitcast.5), custom_call_target="tpu_custom_call" | custom-call | tf_op jit(solution)/shard_map/pick_blocks/pallas_call | solution.py:49
  7.6 0.0 copy-start
  7.6 0.0 copy-start.2
  7.6 0.0 copy-start.1
  7.6 11.6 %all-to-all-start = ((bf16[32,8,12288]{2,1,0:T(8,128)(2,1)}), bf16[32,8,12288]{2,1,0:T(8,128)(2,1)}, u32[]{:S(2)}, u32[]{:S(2)}) async-start(bf16[32,8,12288]{2,1,0:T(8,128)(2,1)} %pick_blocks.1), calls=%async_computation | async-start | bytes 12582912 | tf_op jit(solution)/shard_map/all_to_all | solution.py:504
  19.2 0.0 copy-done
  19.2 0.1 copy.9
  19.4 0.2 rev.3
  19.6 0.0 copy-done.2
  19.6 0.1 pad_dynamic-slice_fusion
  19.7 0.1 slice_compare_fusion
  19.8 0.1 broadcast_dynamic-update-slice_fusion.5
  19.9 0.1 broadcast_dynamic-update-slice_fusion.4
  20.0 0.1 broadcast_dynamic-update-slice_fusion.3
  20.1 0.1 broadcast_dynamic-update-slice_fusion.2
  20.2 0.1 broadcast_dynamic-update-slice_fusion.1
  20.4 0.1 broadcast_dynamic-update-slice_fusion
  20.5 0.9 convert_element_type.16.short_mask
  21.4 0.0 copy-done.1
  21.4 0.8 broadcast_in_dim.16
  22.2 1.8 reshape.97
  24.0 0.8 pad.13.short_full
  24.8 0.8 pad_convert_fusion.base_ref
  25.6 0.1 broadcast_compare_fusion
  25.7 0.7 add_convert_fusion.mask_ref
  26.4 29.4 %build_bands.1.bands = bf16[16,2,2048,256]{3,2,1,0:T(8,128)(2,1)} custom-call(f32[256,256]{1,0:T(8,128)} %pad_convert_fusion.base_ref, f32[2,128,256]{2,1,0:T(8,128)} %add_convert_fusion.mask_ref), custom_call_target="tpu_custom_call" | custom-call | flops 33554432 | bytes 33554432 | tf_op jit(solution)/shard_map/build_bands/pallas_call | solution.py:82
  55.8 43.7 %all-to-all-done = bf16[32,8,12288]{2,1,0:T(8,128)(2,1)} async-done(((bf16[32,8,12288]{2,1,0:T(8,128)(2,1)}), bf16[32,8,12288]{2,1,0:T(8,128)(2,1)}, u32[]{:S(2)}, u32[]{:S(2)}) %all-to-all-start) | async-done | bytes 6291488 | tf_op jit(solution)/shard_map/all_to_all | solution.py:504
  99.5 149.3 %mixer.1 = bf16[256,8192]{1,0:T(8,128)(2,1)} custom-call(bf16[256,12288]{1,0:T(8,128)(2,1)} %bitcast.2.owned, bf16[16,2,2048,256]{3,2,1,0:T(8,128)(2,1)} %build_bands.1.bands, f32[6,256,128]{2,1,0:T(8,128)} %convert_element_type.16.short_mask, f32[8,12288]{1,0:T(8,128)} %pad.13.short_full, bf16[128,2048]{1,0:T(8,128)(2,1)} %weight.1), custom_call_target="tpu_custom_call" | custom-call | tf_op jit(solution)/shard_map/mixer/pallas_call | solution.py:460
  248.8 4.6 %copy.16 = bf16[256,8192]{1,0:T(8,128)(2,1)} copy(bf16[256,8192]{1,0:T(8,128)(2,1)} %mixer.1) | data formatting | bytes 8388608
  (2 shorter events, 0.0 us)
Async XLA Ops:
  7.6 11.6 %copy-start = (bf16[128,256]{1,0:T(8,128)(2,1)S(1)}, bf16[128,256]{1,0:T(8,128)(2,1)}, u32[]{:S(2)}) copy-start(bf16[128,256]{1,0:T(8,128)(2,1)} %param.10) | copy-start | bytes 196612
  7.6 12.0 %copy-start.2 = (s32[1,1024]{1,0:T(1,128)S(1)}, s32[1,1024]{1,0:T(1,128)}, u32[]{:S(2)}) copy-start(s32[1,1024]{1,0:T(1,128)} %param.8) | copy-start | bytes 12292
  7.6 13.8 %copy-start.1 = (f32[7,768]{1,0:T(8,128)S(1)}, f32[7,768]{1,0:T(8,128)}, u32[]{:S(2)}) copy-start(f32[7,768]{1,0:T(8,128)} %param.9) | copy-start | bytes 64516
  7.6 91.8 %all-to-all-start = ((bf16[32,8,12288]{2,1,0:T(8,128)(2,1)}), bf16[32,8,12288]{2,1,0:T(8,128)(2,1)}, u32[]{:S(2)}, u32[]{:S(2)}) async-start(bf16[32,8,12288]{2,1,0:T(8,128)(2,1)} %pick_blocks.1), calls=%async_computation | async-start | bytes 12582912 | tf_op jit(solution)/shard_map/all_to_all | solution.py:504

commit v2 on v1

v2 whole, which is shorter than its diff:
```python
import functools

import jax
import jax.numpy as jnp
from jax import lax
from jax.experimental import pallas as pl
from jax.experimental.pallas import tpu as pltpu
from jax.sharding import PartitionSpec as P

MESH = pl.DeviceIdType.MESH
VMEM_LIMIT = 66_000_000
RING = 4
WAVES = 4
TILE = 256
BLOCK = 128
GROUP = 16
TAPS = 7
CHUNK = 512
BUFFERS = 4


def pick_kernel(route, loaded, picked, held, load_sem, store_sem):
    blocks = loaded.shape[0]
    chunks = picked.shape[0]

    def load(i):
        return pltpu.make_async_copy(loaded.at[i], held.at[i], load_sem.at[i])

    def store(i, k, j):
        column = j * chunks * CHUNK + k * CHUNK
        return pltpu.make_async_copy(
            held.at[i, :, pl.ds(column, CHUNK)],
            picked.at[k, route[0, i], :, pl.ds(j * CHUNK, CHUNK)],
            store_sem.at[i, k, j],
        )

    @pl.loop(0, blocks)
    def _(i):
        load(i).start()

    @pl.loop(0, blocks)
    def _(i):
        load(i).wait()
        for k in range(chunks):
            for j in range(3):
                store(i, k, j).start()

    @pl.loop(0, blocks)
    def _(i):
        for k in range(chunks):
            for j in range(3):
                store(i, k, j).wait()


def pick_blocks(route, loaded):
    blocks, rows, wide = loaded.shape
    chunks = wide // (3 * CHUNK)
    return pl.pallas_call(
        pick_kernel,
        out_shape=jax.ShapeDtypeStruct((chunks, blocks, rows, 3 * CHUNK), loaded.dtype),
        in_specs=[
            pl.BlockSpec(memory_space=pltpu.SMEM),
            pl.BlockSpec(memory_space=pl.ANY),
        ],
        out_specs=pl.BlockSpec(memory_space=pl.ANY),
        scratch_shapes=[
            pltpu.VMEM((blocks, rows, wide), loaded.dtype),
            pltpu.SemaphoreType.DMA((blocks,)),
            pltpu.SemaphoreType.DMA((blocks, chunks, 3)),
        ],
        compiler_params=pltpu.CompilerParams(vmem_limit_bytes=VMEM_LIMIT),
        name="pick_blocks",
    )(route, loaded)


def mixer_kernel(
    picked, doc_ids, short_filter, medium_filter, weight, out,
    w_all, gated, staged, rows, feat, gate, xk, bands,
    taps, short_full, base, id_rows, id_columns, short_mask, band_mask,
    xs, xr, xo,
    ys, yr, d1s, d1r, d2s, d2r, e1s, e1r, e2s, e2r,
    fs, fr, hs, hr, ns, nr, ss, sr, gs, gr, cs, cr, os,
):
    fsdp, ctx = lax.axis_index("fsdp"), lax.axis_index("ctx")
    yh, zc, xc = fsdp // (RING * RING), (fsdp // RING) % RING, fsdp % RING
    sib, nb = (fsdp, ctx ^ 1), (fsdp, ctx ^ 2)
    after, before = (fsdp, (ctx + 1) % 4), (fsdp, (ctx + 3) % 4)
    partner = ((1 - yh) * RING * RING + zc * RING + xc, ctx)
    channels = gated.shape[2]
    tiles = channels // TILE
    chunks = channels // CHUNK
    blocks, blk = rows.shape[1], rows.shape[2]
    tok = blocks * blk

    def coords(h):
        return (xc, zc) if h == 0 else (zc, xc)

    def dev(h, a, b):
        a, b = (a + RING) % RING, (b + RING) % RING
        z, x = (b, a) if h == 0 else (a, b)
        return (yh * RING * RING + z * RING + x, ctx)

    def piece(w, h, y, a, b):
        a, b = (a + RING) % RING, (b + RING) % RING
        z, x = (b, a) if h == 0 else (a, b)
        return w_all.at[w, h, y, z, x]

    def panel(w, h, y, b):
        b = (b + RING) % RING
        if h == 0:
            return w_all.at[w, h, y, b]
        return w_all.at[w, h, y, :, b]

    def panels(w, h, b):
        b = (b + RING) % RING
        if h == 0:
            return w_all.at[w, h, :, b]
        return w_all.at[w, h, :, :, b]

    def shard(w, h):
        return weight.at[:, pl.ds(w * CHUNK + h * TILE, TILE)]

    def remote(src, dst, send, recv, to):
        return pltpu.make_async_remote_copy(
            src_ref=src, dst_ref=dst, send_sem=send, recv_sem=recv, device_id=to, device_id_type=MESH
        )

    halves = [(w, h) for w in range(WAVES) for h in range(2)]
    ways = ((0, 1), (1, -1))

    def y_copy(w, h):
        a, b = coords(h)
        return remote(shard(w, h), piece(w, h, yh, a, b), ys.at[w, h], yr.at[w, h], partner)

    def y_got(w, h):
        a, b = coords(h)
        return remote(shard(w, h), piece(w, h, 1 - yh, a, b), ys.at[w, h], yr.at[w, h], partner)

    def d1_copy(w, h, d, step, other):
        a, b = coords(h)
        y = 1 - yh if other else yh
        src = piece(w, h, y, a, b) if other else shard(w, h)
        return remote(src, piece(w, h, y, a, b), d1s.at[w, h, d, other], d1r.at[w, h, d, other], dev(h, a + step, b))

    def d1_got(w, h, d, step, other):
        a, b = coords(h)
        y = 1 - yh if other else yh
        dst = piece(w, h, y, a - step, b)
        return remote(dst, dst, d1s.at[w, h, d, other], d1r.at[w, h, d, other], dev(h, a + step, b))

    def d2_copy(w, h, d, step):
        a, b = coords(h)
        ref = piece(w, h, d, a - step, b)
        return remote(ref, ref, d2s.at[w, h, d], d2r.at[w, h, d], dev(h, a + step, b))

    def d2_got(w, h, d, step):
        a, b = coords(h)
        ref = piece(w, h, d, a - 2 * step, b)
        return remote(ref, ref, d2s.at[w, h, d], d2r.at[w, h, d], dev(h, a + step, b))

    def e1_copy(w, h, d, step):
        a, b = coords(h)
        return remote(panels(w, h, b), panels(w, h, b), e1s.at[w, h, d], e1r.at[w, h, d], dev(h, a, b + step))

    def e1_got(w, h, d, step):
        a, b = coords(h)
        ref = panels(w, h, b - step)
        return remote(ref, ref, e1s.at[w, h, d], e1r.at[w, h, d], dev(h, a, b + step))

    def e2_copy(w, h, d, step):
        a, b = coords(h)
        ref = panel(w, h, d, b - step)
        return remote(ref, ref, e2s.at[w, h, d], e2r.at[w, h, d], dev(h, a, b + step))

    def e2_got(w, h, d, step):
        a, b = coords(h)
        ref = panel(w, h, d, b - 2 * step)
        return remote(ref, ref, e2s.at[w, h, d], e2r.at[w, h, d], dev(h, a, b + step))

    def own_shard(w, h):
        a, b = coords(h)
        return pltpu.make_async_copy(shard(w, h), piece(w, h, yh, a, b), os.at[w, h])

    def feat_copy(k):
        return remote(rows.at[k, blocks - 1], feat.at[k], fs.at[k], fr.at[k], after)

    def halo_copy(t):
        return remote(
            gate.at[t, pl.ds(tok, BLOCK)], gate.at[t, pl.ds(0, BLOCK)], hs.at[t], hr.at[t], after
        )

    def part(c, k):
        return gated.at[c, :, pl.ds(pl.multiple_of(k * CHUNK, CHUNK), CHUNK)]

    def near_copy(k):
        return remote(part(ctx, k), part(ctx, k), ss.at[k], sr.at[k], sib)

    def near_got(k):
        return remote(part(ctx ^ 1, k), part(ctx ^ 1, k), ss.at[k], sr.at[k], sib)

    def far_copy(k):
        return remote(part(ctx, k), part(ctx, k), ns.at[k], nr.at[k], nb)

    def far_got(k):
        return remote(part(ctx ^ 2, k), part(ctx ^ 2, k), ns.at[k], nr.at[k], nb)

    def hand_copy(k):
        return remote(part(ctx ^ 2, k), part(ctx ^ 2, k), gs.at[k], gr.at[k], sib)

    def hand_got(k):
        return remote(part(ctx ^ 3, k), part(ctx ^ 3, k), gs.at[k], gr.at[k], sib)

    def out_at(c, w, h):
        start = pl.multiple_of(c * (WAVES * CHUNK) + w * CHUNK + h * TILE, TILE)
        return out.at[:, pl.ds(start, TILE)]

    def c_copy(w, h, c):
        return remote(staged.at[w, h, c], out_at(ctx, w, h), cs.at[w, h, c], cr.at[w, h, ctx], (fsdp, c))

    def c_got(w, h, c):
        return remote(staged.at[w, h, c], out_at(c, w, h), cs.at[w, h, c], cr.at[w, h, c], (fsdp, c))

    def c_own(w, h):
        return pltpu.make_async_copy(staged.at[w, h, ctx], out_at(ctx, w, h), cs.at[w, h, ctx])

    others = [(y, z, x) for y in range(2) for z in range(RING) for x in range(RING)][1:]
    others.sort(key=lambda d: (d[0] * 7 + d[1] * 5 + d[2] * 3) % 11)

    def shifted(d):
        z, x = (zc + d[1]) % RING, (xc + d[2]) % RING
        return ((yh + d[0]) % 2) * RING * RING + z * RING + x

    def block_copy(k, d):
        to = shifted(d)
        return remote(picked.at[k, to], rows.at[k, fsdp], xs.at[k], xr.at[k], (to, ctx))

    def block_all(k):
        few = pl.ds(0, len(others))
        return remote(picked.at[k, few], rows.at[k, few], xs.at[k], xr.at[k], partner)

    def block_own(k):
        return pltpu.make_async_copy(picked.at[k, fsdp], rows.at[k, fsdp], xo.at[k])

    barrier = pltpu.get_barrier_semaphore()
    friends = [(shifted(d), ctx) for d in others] + [sib, nb, (fsdp, ctx ^ 3)]
    for friend in friends:
        pl.semaphore_signal(barrier, inc=1, device_id=friend, device_id_type=MESH)
    pl.semaphore_wait(barrier, len(friends))

    @pl.loop(0, chunks)
    def _(k):
        for d in others:
            block_copy(k, d).start()
        block_own(k).start()

    for w, h in halves:
        own_shard(w, h).start()

    start = jnp.maximum(ctx * tok - BLOCK, 0)
    first = doc_ids[:, pl.ds(pl.multiple_of(start, BLOCK), BLOCK)].astype(jnp.float32)
    id_rows[:, 0:BLOCK] = jnp.where(ctx > 0, first, -1.0)
    id_rows[:, BLOCK:] = doc_ids[:, pl.ds(pl.multiple_of(ctx * tok, tok), tok)].astype(jnp.float32)
    for m in range(3):
        spread_ids = jnp.broadcast_to(id_rows[:, m * BLOCK : (m + 1) * BLOCK], (BLOCK, BLOCK))
        id_columns[m * BLOCK : (m + 1) * BLOCK, :] = spread_ids.T
    for i in range(1, TAPS):
        same = id_columns[BLOCK - i : BLOCK - i + tok, :] == id_columns[BLOCK:, :]
        short_mask[i - 1] = same.astype(jnp.float32)
    for b in range(2):
        own_id = id_columns[(b + 1) * BLOCK : (b + 2) * BLOCK, :]
        for m in range(2):
            same = own_id == id_rows[:, (b + m) * BLOCK : (b + m + 1) * BLOCK]
            band_mask[b, :, m * BLOCK : (m + 1) * BLOCK] = same.astype(jnp.float32)
    depth = medium_filter.shape[0]
    tap_row = lax.broadcasted_iota(jnp.int32, (depth, 2 * BLOCK), 0)
    tap_column = lax.broadcasted_iota(jnp.int32, (depth, 2 * BLOCK), 1)
    flip = (tap_row + tap_column == depth).astype(jnp.bfloat16)
    base[...] = lax.dot_general(
        medium_filter[...], flip, (((0,), (0,)), ((), ())), preferred_element_type=jnp.float32
    )
    taps[...] = jnp.zeros_like(taps)
    taps[0:TAPS, :] = short_filter[...]
    group_row = lax.broadcasted_iota(jnp.int32, (BLOCK, CHUNK), 0)
    group_column = lax.broadcasted_iota(jnp.int32, (BLOCK, CHUNK), 1) // GROUP

    @pl.loop(0, 3 * chunks)
    def _(j):
        per = CHUNK // GROUP
        source = pl.multiple_of((j * per // BLOCK) * BLOCK, BLOCK)
        repeat = (group_row == group_column + j * per - source).astype(jnp.float32)
        short_full[:, pl.ds(pl.multiple_of(j * CHUNK, CHUNK), CHUNK)] = jnp.dot(
            taps[:, pl.ds(source, BLOCK)], repeat,
            precision=lax.Precision.HIGHEST, preferred_element_type=jnp.float32,
        )

    def build_bands(t):
        def one(j, carry):
            row = jnp.broadcast_to(base[pl.ds(t * GROUP + j, 1), :], (BLOCK, 2 * BLOCK))
            band = pltpu.roll(row, 0, 1, stride=1, stride_axis=0)
            first_row = pl.multiple_of(j * BLOCK, BLOCK)
            for b in range(2):
                bands[t % BUFFERS, b, pl.ds(first_row, BLOCK), :] = (band * band_mask[b]).astype(jnp.bfloat16)
            return carry

        lax.fori_loop(0, GROUP, one, 0)

    @pl.loop(0, BUFFERS)
    def _(t):
        build_bands(t)

    lane_group = lax.broadcasted_iota(jnp.int32, (BLOCK, TILE), 1) // GROUP

    def expand(slot, k, half, j):
        for l in range(TILE // BLOCK):
            column = pl.multiple_of(j * CHUNK + half * TILE + l * BLOCK, BLOCK)
            xk[slot, l, pl.ds(0, 8), :] = feat[k, :, pl.ds(column, BLOCK)].astype(jnp.float32)
            own = rows[k, :, :, pl.ds(column, BLOCK)].astype(jnp.float32)
            xk[slot, l, pl.ds(8, tok), :] = own.reshape(tok, BLOCK)

    def short(slot, column, b, l):
        total = None
        for i in range(TAPS):
            tap = short_full[i, pl.ds(pl.multiple_of(column + l * BLOCK, BLOCK), BLOCK)][None, :]
            term = xk[slot, l, pl.ds(8 + b * BLOCK - i, BLOCK), :] * tap
            if i > 0:
                term = term * short_mask[i - 1, b * BLOCK : (b + 1) * BLOCK, :]
            total = term if total is None else total + term
        return total

    def make_gate(k, half):
        t = 2 * k + half
        key = pl.multiple_of(channels + t * TILE, TILE)
        value = pl.multiple_of(2 * channels + t * TILE, TILE)
        expand(0, k, half, 1)
        expand(1, k, half, 2)
        for b in range(2):
            for l in range(TILE // BLOCK):
                product = short(0, key, b, l) * short(1, value, b, l)
                gate[t, pl.ds((b + 1) * BLOCK, BLOCK), l * BLOCK : (l + 1) * BLOCK] = product.astype(jnp.bfloat16)
        halo_copy(t).start()

    def convolve(k, half):
        t = 2 * k + half
        query = pl.multiple_of(t * TILE, TILE)
        expand(2, k, half, 0)
        halo_copy(t).wait_recv()
        for b in range(2):
            spread = jnp.dot(
                bands[t % BUFFERS, b], gate[t, pl.ds(b * BLOCK, 2 * BLOCK), :], preferred_element_type=jnp.float32
            )
            medium = spread[0:BLOCK]
            for j in range(1, GROUP):
                medium = jnp.where(lane_group == j, spread[j * BLOCK : (j + 1) * BLOCK], medium)
            for l in range(TILE // BLOCK):
                done = short(2, query, b, l) * medium[:, l * BLOCK : (l + 1) * BLOCK]
                at = pl.multiple_of(query + l * BLOCK, BLOCK)
                gated[ctx, b * BLOCK : (b + 1) * BLOCK, pl.ds(at, BLOCK)] = done.astype(jnp.bfloat16)

        @pl.when(t + BUFFERS < tiles)
        def _():
            build_bands(t + BUFFERS)

    def weight_one():
        for w, h in halves:
            y_copy(w, h).start()
            for d, step in ways:
                d1_copy(w, h, d, step, 0).start()

    def weight_other():
        for w, h in halves:
            y_got(w, h).wait_recv()
            for d, step in ways:
                d1_copy(w, h, d, step, 1).start()

    def weight_two():
        for w, h in halves:
            for d, step in ways:
                d1_got(w, h, d, step, 0).wait_recv()
                d1_got(w, h, d, step, 1).wait_recv()
                d2_copy(w, h, d, step).start()

    def weight_three(w):
        for h in range(2):
            own_shard(w, h).wait()
            for d, step in ways:
                d2_got(w, h, d, step).wait_recv()
        for h in range(2):
            for d, step in ways:
                e1_copy(w, h, d, step).start()

    def weight_four(w):
        for h in range(2):
            for d, step in ways:
                e1_got(w, h, d, step).wait_recv()
                e2_copy(w, h, d, step).start()

    def weight_done(w):
        for h in range(2):
            for d, step in ways:
                e2_got(w, h, d, step).wait_recv()

    def hand_on(k):
        far_got(k).wait_recv()
        hand_copy(k).start()

    @pl.loop(0, chunks + 2)
    def _(k):
        @pl.when(k < chunks)
        def _():
            block_all(k).wait_recv()
            block_own(k).wait()
            feat_copy(k).start()

        @pl.when(k == 4)
        def _():
            weight_one()

        @pl.when(k == 5)
        def _():
            weight_other()

        @pl.when(k == 6)
        def _():
            weight_two()

        @pl.when(k == 7)
        def _():
            weight_three(0)
            weight_three(1)

        @pl.when(k == 8)
        def _():
            weight_three(2)

        @pl.when((k > 0) & (k <= chunks))
        def _():
            feat_copy(k - 1).wait_recv()

            @pl.loop(0, 2)
            def _(half):
                make_gate(k - 1, half)

        @pl.when(k > 1)
        def _():
            @pl.loop(0, 2)
            def _(half):
                convolve(k - 2, half)

            far_copy(k - 2).start()
            near_copy(k - 2).start()

    for k in range(4):
        hand_on(k)
    weight_four(0)
    weight_three(3)
    hand_on(4)
    weight_four(1)
    hand_on(5)
    hand_on(6)
    weight_four(2)
    hand_on(7)
    for k in range(chunks):
        near_got(k).wait_recv()
        hand_got(k).wait_recv()

    mine = ctx // 2

    def multiply(w):
        def one_half(h, carry):
            cols = w_all[w, h].reshape(channels, TILE)
            for far in (1, 0):
                base = 2 * ((mine + far) % 2)
                lhs = gated[pl.ds(base, 2)].reshape(2 * tok, channels)
                product = jnp.dot(lhs, cols, preferred_element_type=jnp.float32)
                staged[w, h, pl.ds(base, 2)] = product.astype(jnp.bfloat16).reshape(2, tok, TILE)
                if far:
                    c_copy(w, h, base).start()
                    c_copy(w, h, base + 1).start()
                else:
                    c_copy(w, h, ctx ^ 1).start()
                    c_own(w, h).start()
            return carry

        lax.fori_loop(0, 2, one_half, 0)

    for w in range(WAVES):
        weight_done(w)
        multiply(w)
        if w == 1:
            weight_four(3)

    for k in range(chunks):
        block_all(k).wait_send()
        feat_copy(k).wait_send()
    for w, h in halves:
        y_copy(w, h).wait_send()
        for d, step in ways:
            for other in range(2):
                d1_copy(w, h, d, step, other).wait_send()
            d2_copy(w, h, d, step).wait_send()
            e1_copy(w, h, d, step).wait_send()
            e2_copy(w, h, d, step).wait_send()
    for t in range(tiles):
        halo_copy(t).wait_send()
    for k in range(chunks):
        far_copy(k).wait_send()
        near_copy(k).wait_send()
        hand_copy(k).wait_send()
    for w, h in halves:
        c_own(w, h).wait()
        for flip in (1, 2, 3):
            c_copy(w, h, ctx ^ flip).wait_send()
            c_got(w, h, ctx ^ flip).wait_recv()


def mix(picked, doc_ids, short_filter, medium_filter, weight):
    chunks, blocks, blk, triple = picked.shape
    tok, channels = blocks * blk, chunks * triple // 3
    depth, columns = weight.shape
    tiles, groups = channels // TILE, medium_filter.shape[1]
    dma = pltpu.SemaphoreType.DMA
    vmem, anywhere = pl.BlockSpec(memory_space=pltpu.VMEM), pl.BlockSpec(memory_space=pl.ANY)
    return pl.pallas_call(
        mixer_kernel,
        out_shape=jax.ShapeDtypeStruct((tok, 4 * columns), jnp.bfloat16),
        in_specs=[anywhere, vmem, vmem, vmem, anywhere],
        out_specs=anywhere,
        scratch_shapes=[
            pltpu.VMEM((WAVES, 2, 2, RING, RING, depth, TILE), jnp.bfloat16),
            pltpu.VMEM((4, tok, channels), jnp.bfloat16),
            pltpu.VMEM((WAVES, 2, 4, tok, TILE), jnp.bfloat16),
            pltpu.VMEM(picked.shape, jnp.bfloat16),
            pltpu.VMEM((chunks, blk, triple), jnp.bfloat16),
            pltpu.VMEM((tiles, tok + BLOCK, TILE), jnp.bfloat16),
            pltpu.VMEM((3, TILE // BLOCK, tok + 8, BLOCK), jnp.float32),
            pltpu.VMEM((BUFFERS, 2, GROUP * BLOCK, 2 * BLOCK), jnp.bfloat16),
            pltpu.VMEM((8, short_filter.shape[1]), jnp.float32),
            pltpu.VMEM((8, 3 * channels), jnp.float32),
            pltpu.VMEM((groups, 2 * BLOCK), jnp.float32),
            pltpu.VMEM((1, 3 * BLOCK), jnp.float32),
            pltpu.VMEM((3 * BLOCK, BLOCK), jnp.float32),
            pltpu.VMEM((TAPS - 1, tok, BLOCK), jnp.float32),
            pltpu.VMEM((2, BLOCK, 2 * BLOCK), jnp.float32),
            dma((chunks,)), dma((chunks,)), dma((chunks,)),
            dma((WAVES, 2)), dma((WAVES, 2)),
            dma((WAVES, 2, 2, 2)), dma((WAVES, 2, 2, 2)),
            dma((WAVES, 2, 2)), dma((WAVES, 2, 2)),
            dma((WAVES, 2, 2)), dma((WAVES, 2, 2)),
            dma((WAVES, 2, 2)), dma((WAVES, 2, 2)),
            dma((chunks,)), dma((chunks,)),
            dma((tiles,)), dma((tiles,)),
            dma((chunks,)), dma((chunks,)),
            dma((chunks,)), dma((chunks,)),
            dma((chunks,)), dma((chunks,)),
            dma((WAVES, 2, 4)), dma((WAVES, 2, 4)),
            dma((WAVES, 2)),
        ],
        compiler_params=pltpu.CompilerParams(
            vmem_limit_bytes=VMEM_LIMIT, collective_id=0, has_side_effects=True
        ),
        name="mixer",
    )(picked, doc_ids, short_filter, medium_filter, weight)


def on_device(loaded, route, doc_ids, short_filter, medium_filter, out_weight):
    tok, wide = loaded.shape
    blocks = route.shape[1]
    picked = pick_blocks(route, loaded.reshape(blocks, tok // blocks, wide))
    return mix(picked, doc_ids, short_filter, medium_filter, out_weight)


def solution(mesh):
    placed = (
        P(("fsdp", "ctx"), None),
        P(("fsdp", "ctx"), None),
        P("fsdp", None),
        P(),
        P(),
        P("fsdp", "ctx"),
    )
    return jax.shard_map(
        on_device, mesh=mesh, in_specs=placed, out_specs=P(("fsdp", "ctx"), None), check_vma=False
    )
```

time: 254 us -> 237 us (0.933)
  Pallas kernels: 185 us -> 232 us
  waiting for transfers between devices: 43.7 us -> 0 us
  starting transfers between devices: 11.6 us -> 0 us
  local copies, waits for them, and re-layouts: 9.09 us -> 4.64 us
  other arithmetic: 3.97 us -> 0 us
    pallas_call x1, Pallas kernels: 149 us -> 218 us  [mix(): pl.pallas_call(mixer_kernel, out_shape=jax.ShapeDtypeStruct((tok, 4 * col...]
    all_to_all x1 -> x0, waiting for transfers between devices: 43.7 us -> none  [on_device(): lax.all_to_all(picked, 'fsdp', split_axis=0, concat_axis=0, tiled=True)]
    pallas_call x2 -> x1, Pallas kernels: 35.7 us -> 13.6 us  [pick_blocks(): pl.pallas_call(pick_kernel, out_shape=jax.ShapeDtypeStruct((chunks, block...]
    all_to_all x1 -> x0, starting transfers between devices: 11.6 us -> none  [on_device(): lax.all_to_all(picked, 'fsdp', split_axis=0, concat_axis=0, tiled=True)]
    unnamed x13 -> x1, local copies, waits for them, and re-layouts: 5.34 us -> 4.64 us
  transfers between devices with their start and end apart: 1 -> 0, of which waited for: 1 -> 0; matrix products, arithmetic and copies ran while one was open for 3% -> 0% of each run, Pallas kernels for 12% -> 0%
where the time goes in v2:
time: 237 us; the launch traced here: 236 us
  Pallas kernels  232 us (98%)
  local copies, waits for them, and re-layouts  4.64 us (2%)
    pallas_call x1, Pallas kernels, mix(): pl.pallas_call(mixer_kernel, out_shape=jax.ShapeDtypeStruct((tok, 4 * col...  218 us
    pallas_call x1, Pallas kernels, pick_blocks(): pl.pallas_call(pick_kernel, out_shape=jax.ShapeDtypeStruct((chunks, block...  13.6 us

profile of v2, /device:TPU:1, one launch (start us, length us, event | category | flops | bytes accessed | tf_op | source)
XLA Modules:
  0.0 236.4 jit_solution(13172581469682368477)
XLA Ops:
  0.0 13.6 %pick_blocks.1.picked = bf16[8,32,8,1536]{3,2,1,0:T(8,128)(2,1)} custom-call(s32[1,32]{1,0:T(1,128)} %route.1, bf16[32,8,12288]{2,1,0:T(8,128)(2,1)} %bitcast.1), custom_call_target="tpu_custom_call" | custom-call | tf_op jit(solution)/shard_map/pick_blocks/pallas_call | solution.py:58
  13.6 218.1 %mixer.1 = bf16[256,8192]{1,0:T(8,128)(2,1)} custom-call(bf16[8,32,8,1536]{3,2,1,0:T(8,128)(2,1)} %pick_blocks.1.picked, s32[1,1024]{1,0:T(1,128)} %doc_ids.1, f32[7,768]{1,0:T(8,128)} %short_filter.1, bf16[128,256]{1,0:T(8,128)(2,1)} %medium_filter.1, bf16[128,2048]{1,0:T(8,128)(2,1)} %weight.1), custom_call_target="tpu_custom_call" | custom-call | tf_op jit(solution)/shard_map/mixer/pallas_call | solution.py:523
  231.7 4.6 %copy.8 = bf16[256,8192]{1,0:T(8,128)(2,1)} copy(bf16[256,8192]{1,0:T(8,128)(2,1)} %mixer.1) | data formatting | bytes 8388608
